TPU v7x, 32 devices: a whole 2x2x4 slice. The times are simulated.
32 devices in a mesh: dp: 8 (over z, y), tensor: 4 (over x, core).
Axes of the slice: x: 2, y: 2, z: 4, core: 2. Of those that a mesh axis runs over, the one named last changes fastest.
Arguments:
- tokens: bfloat16 [16384, 1536], P(('dp', 'tensor')), may hold values from -6 to 6
- segments: int32 [16384], P('dp'), may hold values from 0 to 3, as said below
- positions: int32 [16384], P('dp'), may hold values from 0 to 2044, as said below
- norm_attn: float32 [1536], replicated, may hold values from 0.1 to 1.9
- w_query: bfloat16 [1536, 1536], P(None, 'tensor'), may hold values from -0.15625 to 0.15625
- key_weight: bfloat16 [1536, 768], P(None, 'tensor'), may hold values from -0.15625 to 0.15625
- value_weight: bfloat16 [1536, 768], P(None, 'tensor'), may hold values from -0.15625 to 0.15625
- w_out: bfloat16 [1536, 1536], P('tensor'), may hold values from -1.5 to 1.5
- norm_mlp: float32 [1536], replicated, may hold values from 0.1 to 1.9
- w_gate: bfloat16 [1536, 4096], P(None, 'tensor'), may hold values from -0.15625 to 0.15625
- w_up: bfloat16 [1536, 4096], P(None, 'tensor'), may hold values from -0.15625 to 0.15625
- w_down: bfloat16 [4096, 1536], P('tensor'), may hold values from -0.09375 to 0.09375
- cotangent: bfloat16 [16384, 1536], P(('dp', 'tensor')), may hold values from -6 to 6
Outputs:
- output: bfloat16 [16384, 1536], P(('dp', 'tensor'))
- grad_tokens: float32 [16384, 1536], P(('dp', 'tensor'))
- grad_norm_attn: float32 [1536], replicated
- grad_w_query: float32 [1536, 1536], P(None, 'tensor')
- grad_w_key: float32 [1536, 768], P(None, 'tensor')
- grad_w_value: float32 [1536, 768], P(None, 'tensor')
- grad_w_out: float32 [1536, 1536], P('tensor')
- grad_norm_mlp: float32 [1536], replicated
- grad_w_gate: float32 [1536, 4096], P(None, 'tensor')
- grad_w_up: float32 [1536, 4096], P(None, 'tensor')
- grad_w_down: float32 [4096, 1536], P('tensor')
Inputs may be any that keep to these rules, and one draw needn't show every extreme that they name: `segments`: within each sequence of 2048 tokens the document numbers never fall, start at 0 and end at 3, each document one token or more. `positions`: each token's position within its document, 0 at the document's first token; the first sequence holds a document of 2045 tokens.
All inputs are finite; a program needn't handle non-finite values.
Results may differ from a plain program's by a relative error of at most 0.018.
Values may be sent and summed in bfloat16 or wider, within the bound.
A program may use at most 256 MiB of HBM per device.

v0:
```python
import math
import jax
import jax.numpy as jnp
from jax import lax
from jax.sharding import PartitionSpec as P

HEAD_SIZE = 96
epsilon = 1e-05
rope_base = 100000.0
masked_value = -1e30


def angle_tables(positions, width):
    middle = width // 2
    freq_steps = jnp.arange(middle, dtype=jnp.float32)
    inverse = jnp.exp(freq_steps * (-2.0 * math.log(rope_base) / width))
    angles = positions.astype(jnp.float32)[:, None] * inverse[None, :]
    return (jnp.cos(angles)[:, None, :], jnp.sin(angles)[:, None, :])


def apply_rotary(values, cosine_lookup, sine_lookup):
    middle = values.shape[-1] // 2
    front, second = (values[..., :middle], values[..., middle:])
    return jnp.concatenate(
        [
            front * cosine_lookup - second * sine_lookup,
            second * cosine_lookup + front * sine_lookup,
        ],
        axis=-1,
    )


def rotate_back(grads_in, cosine_lookup, sine_lookup):
    middle = grads_in.shape[-1] // 2
    front, second = (grads_in[..., :middle], grads_in[..., middle:])
    return jnp.concatenate(
        [
            front * cosine_lookup + second * sine_lookup,
            second * cosine_lookup - front * sine_lookup,
        ],
        axis=-1,
    )


def rms_inverse(values):
    return lax.rsqrt(jnp.mean(values * values, axis=-1, keepdims=True) + epsilon)


def norm_back(grad_normed, gain, unit_rows, inverse):
    scaled = grad_normed * gain
    return inverse * (scaled - unit_rows * jnp.mean(scaled * unit_rows, axis=-1, keepdims=True))


def contract_rows(left, right):
    return lax.dot_general(
        left, right, (((0,), (0,)), ((), ())), preferred_element_type=jnp.float32
    )


def contract_cols(left, right):
    return lax.dot_general(
        left, right, (((1,), (1,)), ((), ())), preferred_element_type=jnp.float32
    )


def block_scores(query_block, heads_of_key, allowed, score_scale):
    scores = (
        jnp.einsum("qgrd,kgd->grqk", query_block, heads_of_key, preferred_element_type=jnp.float32)
        * score_scale
    )
    return jnp.where(allowed[None, None], scores, masked_value)


def body(
    tokens,
    segments,
    positions,
    norm_attn,
    w_query,
    key_weight,
    value_weight,
    w_out,
    norm_mlp,
    w_gate,
    w_up,
    w_down,
    cotangent,
):
    sequence_length = segments.shape[0]
    q_heads = w_query.shape[1] // HEAD_SIZE
    kv_heads = key_weight.shape[1] // HEAD_SIZE
    head_repetitions = q_heads // kv_heads
    score_scale = 1.0 / math.sqrt(HEAD_SIZE)
    rows_per_block = min(512, sequence_length)
    block_total = sequence_length // rows_per_block
    cosine_lookup, sine_lookup = angle_tables(positions, HEAD_SIZE)
    indices = jnp.arange(sequence_length, dtype=jnp.int32)
    seg_blocks = segments.reshape(block_total, rows_per_block)
    index_blocks = indices.reshape(block_total, rows_per_block)
    inputs = tokens.astype(jnp.float32)
    inverse_one = rms_inverse(inputs)
    unit_one = inputs * inverse_one
    first_normalized = (unit_one * norm_attn).astype(jnp.bfloat16)
    attn_in = lax.all_gather(first_normalized, "tensor", axis=0, tiled=True)
    query_proj = jnp.dot(attn_in, w_query, preferred_element_type=jnp.float32).reshape(
        sequence_length, q_heads, HEAD_SIZE
    )
    key_proj = jnp.dot(attn_in, key_weight, preferred_element_type=jnp.float32).reshape(
        sequence_length, kv_heads, HEAD_SIZE
    )
    query_rows = apply_rotary(query_proj, cosine_lookup, sine_lookup).astype(jnp.bfloat16)
    heads_of_key = apply_rotary(key_proj, cosine_lookup, sine_lookup).astype(jnp.bfloat16)
    heads_of_value = (
        jnp.dot(attn_in, value_weight, preferred_element_type=jnp.float32)
        .astype(jnp.bfloat16)
        .reshape(sequence_length, kv_heads, HEAD_SIZE)
    )
    blocks_of_query = query_rows.reshape(
        block_total, rows_per_block, kv_heads, head_repetitions, HEAD_SIZE
    )

    def attend(member):
        query_block, rows_seg, rows_idx = member
        allowed = (rows_seg[:, None] == segments[None, :]) & (indices[None, :] <= rows_idx[:, None])
        scores = block_scores(query_block, heads_of_key, allowed, score_scale)
        row_peak = jnp.max(scores, axis=-1, keepdims=True)
        weights = jnp.exp(scores - row_peak)
        totals = jnp.sum(weights, axis=-1, keepdims=True)
        weights_low = (weights / totals).astype(jnp.bfloat16)
        mixed_heads = jnp.einsum(
            "grqk,kgd->qgrd", weights_low, heads_of_value, preferred_element_type=jnp.float32
        )
        return (mixed_heads.astype(jnp.bfloat16), row_peak[..., 0] + jnp.log(totals[..., 0]))

    attended, log_totals = lax.map(attend, (blocks_of_query, seg_blocks, index_blocks))
    attended = attended.reshape(sequence_length, q_heads * HEAD_SIZE)
    row_slice = attended
    attn_out = lax.psum_scatter(
        jnp.dot(row_slice, w_out, preferred_element_type=jnp.float32),
        "tensor",
        scatter_dimension=0,
        tiled=True,
    )
    hidden_one = inputs + attn_out
    inverse_two = rms_inverse(hidden_one)
    unit_two = hidden_one * inverse_two
    normed_two = (unit_two * norm_mlp).astype(jnp.bfloat16)
    mlp_in = lax.all_gather(normed_two, "tensor", axis=0, tiled=True)
    gate_proj = jnp.dot(mlp_in, w_gate, preferred_element_type=jnp.float32)
    up_proj = jnp.dot(mlp_in, w_up, preferred_element_type=jnp.float32)
    sigmoid_gate = jax.nn.sigmoid(gate_proj)
    activated = gate_proj * sigmoid_gate
    hidden = (activated * up_proj).astype(jnp.bfloat16)
    row_slice = hidden
    mlp_out = lax.psum_scatter(
        jnp.dot(row_slice, w_down, preferred_element_type=jnp.float32).astype(jnp.bfloat16),
        "tensor",
        scatter_dimension=0,
        tiled=True,
    ).astype(jnp.float32)
    output = (hidden_one + mlp_out).astype(jnp.bfloat16)
    grad_out = lax.all_gather(cotangent, "tensor", axis=0, tiled=True)
    grad_w_down = contract_rows(hidden, grad_out)
    grad_hidden = contract_cols(grad_out, w_down)
    grad_gate = (
        grad_hidden * up_proj * sigmoid_gate * (1.0 + gate_proj * (1.0 - sigmoid_gate))
    ).astype(jnp.bfloat16)
    grad_upper = (grad_hidden * activated).astype(jnp.bfloat16)
    grad_w_gate = contract_rows(mlp_in, grad_gate)
    grad_w_up = contract_rows(mlp_in, grad_upper)
    grad_normed_two = lax.psum_scatter(
        contract_cols(grad_gate, w_gate) + contract_cols(grad_upper, w_up),
        "tensor",
        scatter_dimension=0,
        tiled=True,
    )
    grad_norm_mlp = jnp.sum(grad_normed_two * unit_two, axis=0)
    grad_hidden_one = cotangent.astype(jnp.float32) + norm_back(
        grad_normed_two, norm_mlp, unit_two, inverse_two
    )
    grad_attn_rows = lax.all_gather(
        grad_hidden_one.astype(jnp.bfloat16), "tensor", axis=0, tiled=True
    )
    grad_w_out = contract_rows(attended, grad_attn_rows)
    grad_attended = contract_cols(grad_attn_rows, w_out).astype(jnp.bfloat16)
    grad_blocks = grad_attended.reshape(
        block_total, rows_per_block, kv_heads, head_repetitions, HEAD_SIZE
    )

    def attend_back(running, member):
        query_block, grad_block, rows_seg, rows_idx, log_block = member
        allowed = (rows_seg[:, None] == segments[None, :]) & (indices[None, :] <= rows_idx[:, None])
        scores = block_scores(query_block, heads_of_key, allowed, score_scale)
        weights = jnp.exp(scores - log_block[..., None])
        grad_weights = jnp.einsum(
            "qgrd,kgd->grqk", grad_block, heads_of_value, preferred_element_type=jnp.float32
        )
        inner_sum = jnp.sum(weights * grad_weights, axis=-1, keepdims=True)
        grad_scores = (weights * (grad_weights - inner_sum)).astype(jnp.bfloat16)
        grad_query = (
            jnp.einsum(
                "grqk,kgd->qgrd", grad_scores, heads_of_key, preferred_element_type=jnp.float32
            )
            * score_scale
        )
        grad_keys = (
            running[0]
            + jnp.einsum(
                "grqk,qgrd->kgd", grad_scores, query_block, preferred_element_type=jnp.float32
            )
            * score_scale
        )
        grad_values = running[1] + jnp.einsum(
            "grqk,qgrd->kgd",
            weights.astype(jnp.bfloat16),
            grad_block,
            preferred_element_type=jnp.float32,
        )
        return ((grad_keys, grad_values), grad_query)

    zero_state = jnp.zeros((sequence_length, kv_heads, HEAD_SIZE), jnp.float32)
    (grad_keys, grad_values), grad_queries = lax.scan(
        attend_back,
        (zero_state, zero_state),
        (blocks_of_query, grad_blocks, seg_blocks, index_blocks, log_totals),
    )
    grad_queries = grad_queries.reshape(sequence_length, q_heads, HEAD_SIZE)
    grad_q_proj = (
        rotate_back(grad_queries, cosine_lookup, sine_lookup)
        .reshape(sequence_length, q_heads * HEAD_SIZE)
        .astype(jnp.bfloat16)
    )
    grad_k_proj = (
        rotate_back(grad_keys, cosine_lookup, sine_lookup)
        .reshape(sequence_length, kv_heads * HEAD_SIZE)
        .astype(jnp.bfloat16)
    )
    grad_v_proj = grad_values.reshape(sequence_length, kv_heads * HEAD_SIZE).astype(jnp.bfloat16)
    grad_w_query = contract_rows(attn_in, grad_q_proj)
    grad_w_key = contract_rows(attn_in, grad_k_proj)
    grad_w_value = contract_rows(attn_in, grad_v_proj)
    grad_normed_one = lax.psum_scatter(
        (
            contract_cols(grad_q_proj, w_query)
            + contract_cols(grad_k_proj, key_weight)
            + contract_cols(grad_v_proj, value_weight)
        ).astype(jnp.bfloat16),
        "tensor",
        scatter_dimension=0,
        tiled=True,
    ).astype(jnp.float32)
    grad_norm_attn = jnp.sum(grad_normed_one * unit_one, axis=0)
    grad_tokens = grad_hidden_one + norm_back(grad_normed_one, norm_attn, unit_one, inverse_one)
    grad_norm_attn, grad_norm_mlp = lax.psum((grad_norm_attn, grad_norm_mlp), ("dp", "tensor"))
    grad_w_query, grad_w_key, grad_w_value, grad_w_out, grad_w_gate, grad_w_up, grad_w_down = (
        lax.psum(grad_w_query.astype(jnp.bfloat16), "dp").astype(jnp.float32),
        lax.psum(grad_w_key.astype(jnp.bfloat16), "dp").astype(jnp.float32),
        lax.psum(grad_w_value.astype(jnp.bfloat16), "dp").astype(jnp.float32),
        lax.psum(grad_w_out.astype(jnp.bfloat16), "dp").astype(jnp.float32),
        lax.psum(grad_w_gate.astype(jnp.bfloat16), "dp").astype(jnp.float32),
        lax.psum(grad_w_up.astype(jnp.bfloat16), "dp").astype(jnp.float32),
        lax.psum(grad_w_down.astype(jnp.bfloat16), "dp").astype(jnp.float32),
    )
    return (
        output,
        grad_tokens,
        grad_norm_attn,
        grad_w_query,
        grad_w_key,
        grad_w_value,
        grad_w_out,
        grad_norm_mlp,
        grad_w_gate,
        grad_w_up,
        grad_w_down,
    )


def solution(mesh):
    in_specs = (
        P(("dp", "tensor"), None),
        P("dp"),
        P("dp"),
        P(),
        P(None, "tensor"),
        P(None, "tensor"),
        P(None, "tensor"),
        P("tensor", None),
        P(),
        P(None, "tensor"),
        P(None, "tensor"),
        P("tensor", None),
        P(("dp", "tensor"), None),
    )
    out_specs = (
        P(("dp", "tensor"), None),
        P(("dp", "tensor"), None),
        P(),
        P(None, "tensor"),
        P(None, "tensor"),
        P(None, "tensor"),
        P("tensor", None),
        P(),
        P(None, "tensor"),
        P(None, "tensor"),
        P("tensor", None),
    )
    return jax.shard_map(body, mesh=mesh, in_specs=in_specs, out_specs=out_specs, check_vma=False)
```

profile of v0, /device:TPU:0, one launch (start us, length us, event | category | flops | bytes accessed | tf_op | source)
XLA Modules:
  0.0 1461.6 jit_solution(5925052065785356915)
XLA Ops:
  15.7 46.3 %all-gather.5.cloned.1.call-done = bf16[2048,1536]{1,0:T(8,128)(2,1)} async-done(((bf16[512,1536]{1,0:T(8,128)(2,1)}), bf16[2048,1536]{1,0:T(8,128)(2,1)}) %all-gather.5.cloned.1.call-update) | async-done | bytes 6291472 | tf_op jit(solution)/shard_map/all_gather | solution.py:104
  89.8 66.6 %while.28 = (s32[]{:T(128)}, bf16[4,512,2,2,96]{1,4,3,2,0:T(8,128)(2,1)}, f32[4,2,2,512]{3,2,1,0:T(2,128)}, s32[4,512]{1,0:T(4,128)S(1)}, s32[2048]{0:T(1024)S(1...) while((s32[]{:T(128)}, ...), condition=%wide.region_4.5_spmd.clone, body=%wide.region_1.4_spmd.clone.sunk | while | flops 1664284672 | bytes 60117144 | solution.py:135
  167.2 99.1 %reduce-scatter.5.cloned.1.call-done = f32[512,1536]{1,0:T(8,128)} async-done(((f32[2048,1536]{1,0:T(8,128)}), f32[512,1536]{1,0:T(8,128)}) %reduce-scatter.5.cloned.1.call-update) | async-done | bytes 3145744 | tf_op jit(solution)/shard_map/reduce_scatter | solution.py:138
  273.0 45.9 %all-gather.7.cloned.1.call-done = bf16[2048,1536]{1,0:T(8,128)(2,1)} async-done(((bf16[512,1536]{1,0:T(8,128)(2,1)}), bf16[2048,1536]{1,0:T(8,128)(2,1)}) %all-gather.7.cloned.1.call-update) | async-done | bytes 6291472 | tf_op jit(solution)/shard_map/all_gather | solution.py:148
  318.9 12.6 fusion.74
  331.5 8.8 fusion.73
  340.3 26.4 %all-gather.9.cloned.1.call-done = bf16[2048,1536]{1,0:T(8,128)(2,1)} async-done(((bf16[512,1536]{1,0:T(8,128)(2,1)}), bf16[2048,1536]{1,0:T(8,128)(2,1)}) %all-gather.9.cloned.1.call-update) | async-done | bytes 6291472 | tf_op jit(solution)/shard_map/all_gather | solution.py:162
  366.8 18.8 %multiply_convert_fusion = (bf16[2048,1024]{1,0:T(8,128)(2,1)}, bf16[2048,1024]{1,0:T(8,128)(2,1)}, bf16[2048,1024]{1,0:T(8,128)(2,1)}) fusion(f32[2048,1024]{1,0:T(8,128)} %fusion.73, f32[2048,1024]{1,0:T(8,128)} %fusion.74, bf16[2048,1536]{1,0:T(8,128)(2,1)} %all-gather.9.cloned.1.call-done, bf16[1024,1536]{1,0:T(8,128)(2,1)S(1)} %copy-done), kind=kOutput, calls=%fused_computation.69 | convolution fusion | flops 6473908224 | bytes 38797312 | tf_op jit(solution)/shard_map/dot_general | solution.py:61
  385.6 11.6 fusion.75
  397.2 12.9 convolution_add_fusion
  410.1 99.1 %reduce-scatter.9.cloned.1.call-done = f32[512,1536]{1,0:T(8,128)} async-done(((f32[2048,1536]{1,0:T(8,128)}), f32[512,1536]{1,0:T(8,128)}) %reduce-scatter.9.cloned.1.call-update) | async-done | bytes 3145744 | tf_op jit(solution)/shard_map/reduce_scatter | solution.py:171
  517.6 46.5 %all-gather.11.cloned.1.call-done = bf16[2048,1536]{1,0:T(8,128)(2,1)} async-done(((bf16[512,1536]{1,0:T(8,128)(2,1)}), bf16[2048,1536]{1,0:T(8,128)(2,1)}) %all-gather.11.cloned.1.call-update) | async-done | bytes 6291472 | tf_op jit(solution)/shard_map/all_gather | solution.py:181
  584.7 274.0 %while.29 = (s32[]{:T(128)}, f32[2048,2,96]{0,2,1:T(8,128)}, f32[2048,2,96]{0,2,1:T(8,128)}, f32[4,512,2,2,96]{1,0,4,3,2:T(4,128)}, bf16[4,512,2,2,96]{1,4,3,2,0...) while((s32[]{:T(128)}, f32[2048,2,96]{0,2,1:T(8,128)}, ...), condition=%wide.region_12.13_spmd.clone, body=%wide.region_10.12_spmd.clone.sunk | while | flops 4094752768 | bytes 214511840 | solution.py:222
  603.6 12.6 fusion.155
  616.3 12.2 fusion.156
  636.6 16.1 %dynamic_update_slice.22 = f32[4,512,2,2,96]{1,0,4,3,2:T(4,128)} dynamic-update-slice(f32[4,512,2,2,96]{1,0,4,3,2:T(4,128)} %get-tuple-element.503, f32[1,512,2,2,96]{1,0,4,3,2:T(1,128)} %copy.49, s32[]{:T(128)S(6)} %copy.66, s32[]{:T(128)} %constant.58.clone.1..sunk, s32[]{:T(128)} %constant.58.clone.1..sunk, s32[]{:T(128)} %constant.58.clone.1..sunk, s32[]{:T(128)} %constant.58.clone.1..sunk) | dynamic-update-slice | bytes 1572868 | tf_op jit(solution)/shard_map/while/body/jit(dynamic_update_index_in_dim)/dynamic_update_slice | solution.py:222
  671.7 12.6 fusion.155
  684.3 12.2 fusion.156
  705.2 16.1 %dynamic_update_slice.22 = f32[4,512,2,2,96]{1,0,4,3,2:T(4,128)} dynamic-update-slice(f32[4,512,2,2,96]{1,0,4,3,2:T(4,128)} %get-tuple-element.503, f32[1,512,2,2,96]{1,0,4,3,2:T(1,128)} %copy.49, s32[]{:T(128)S(6)} %copy.66, s32[]{:T(128)} %constant.58.clone.1..sunk, s32[]{:T(128)} %constant.58.clone.1..sunk, s32[]{:T(128)} %constant.58.clone.1..sunk, s32[]{:T(128)} %constant.58.clone.1..sunk) | dynamic-update-slice | bytes 1572868 | tf_op jit(solution)/shard_map/while/body/jit(dynamic_update_index_in_dim)/dynamic_update_slice | solution.py:222
  740.3 12.6 fusion.155
  753.0 12.2 fusion.156
  773.8 16.1 %dynamic_update_slice.22 = f32[4,512,2,2,96]{1,0,4,3,2:T(4,128)} dynamic-update-slice(f32[4,512,2,2,96]{1,0,4,3,2:T(4,128)} %get-tuple-element.503, f32[1,512,2,2,96]{1,0,4,3,2:T(1,128)} %copy.49, s32[]{:T(128)S(6)} %copy.66, s32[]{:T(128)} %constant.58.clone.1..sunk, s32[]{:T(128)} %constant.58.clone.1..sunk, s32[]{:T(128)} %constant.58.clone.1..sunk, s32[]{:T(128)} %constant.58.clone.1..sunk) | dynamic-update-slice | bytes 1572868 | tf_op jit(solution)/shard_map/while/body/jit(dynamic_update_index_in_dim)/dynamic_update_slice | solution.py:222
  809.0 12.6 fusion.155
  821.6 12.2 fusion.156
  842.5 16.1 %dynamic_update_slice.22 = f32[4,512,2,2,96]{1,0,4,3,2:T(4,128)} dynamic-update-slice(f32[4,512,2,2,96]{1,0,4,3,2:T(4,128)} %get-tuple-element.503, f32[1,512,2,2,96]{1,0,4,3,2:T(1,128)} %copy.49, s32[]{:T(128)S(6)} %copy.66, s32[]{:T(128)} %constant.58.clone.1..sunk, s32[]{:T(128)} %constant.58.clone.1..sunk, s32[]{:T(128)} %constant.58.clone.1..sunk, s32[]{:T(128)} %constant.58.clone.1..sunk) | dynamic-update-slice | bytes 1572868 | tf_op jit(solution)/shard_map/while/body/jit(dynamic_update_index_in_dim)/dynamic_update_slice | solution.py:222
  883.0 12.8 add_convert_fusion
  895.9 10.9 convolution_convert_fusion
  906.9 12.0 convolution_convert_fusion.2
  919.0 10.1 convolution_convert_fusion.3
  957.3 40.1 %all-reduce = (f32[1536]{0:T(1024)}, f32[1536]{0:T(1024)}) all-reduce(f32[1536]{0:T(1024)S(1)} %get-tuple-element.234, f32[1536]{0:T(1024)S(1)} %copy-done.41), channel_id=1, replica_groups=mesh['dp'=8,'tensor'=4] {'dp','tensor'}, use_global_device_ids=true, to_apply=%region_16.17 | all-reduce | flops 3072 | bytes 24576 | tf_op jit(solution)/shard_map/psum | solution.py:254
  997.4 19.3 %reduce-scatter.7.cloned.1.call-done = bf16[512,1536]{1,0:T(8,128)(2,1)} async-done(((bf16[2048,1536]{1,0:T(8,128)(2,1)}), bf16[512,1536]{1,0:T(8,128)(2,1)}) %reduce-scatter.7.cloned.1.call-update) | async-done | bytes 1572880 | tf_op jit(solution)/shard_map/reduce_scatter | solution.py:155
  1023.7 413.4 %all-reduce.4.cloned.1.call-done = (bf16[1536,384]{1,0:T(8,128)(2,1)}, bf16[1536,192]{0,1:T(8,128)(2,1)}, bf16[1536,192]{0,1:T(8,128)(2,1)}, bf16[384,1536]{1,0:...) async-done(((bf16[1536,384]{1,0:T(8,128)(2,1)}, bf16[1536,192]{0,1:T(8,128)(2,1)}, bf16[1536,192]{0,1:T(8,128)(2,1)}, ...) | async-done | bytes 12976144 | tf_op jit(solution)/shard_map/psum | solution.py:256
  (276 shorter events, 335.2 us)
Async XLA Ops:
  7.2 359.6 %copy-start = (bf16[1024,1536]{1,0:T(8,128)(2,1)S(1)}, bf16[1024,1536]{1,0:T(8,128)(2,1)}, u32[]{:S(2)}) copy-start(bf16[1024,1536]{1,0:T(8,128)(2,1)} %param.28) | copy-start | bytes 9437188
  7.2 54.8 %all-gather.5.cloned.1.call-start = ((), (), s32[]{:S(2)}) async-start(), calls=%async_computation.4 | async-start | bytes 7864320 | tf_op jit(solution)/shard_map/all_gather | solution.py:104
  12.8 253.6 %reduce-scatter.5.cloned.1.call-start = ((), (), s32[]{:S(2)}) async-start(), calls=%async_computation.5 | async-start | bytes 15728640 | tf_op jit(solution)/shard_map/reduce_scatter | solution.py:138
  15.7 55.7 %copy-start.7 = (f32[2048,48]{0,1:T(8,128)}, f32[2048,48]{0,1:T(8,128)S(1)}, u32[]{:S(2)}) copy-start(f32[2048,48]{0,1:T(8,128)S(1)} %get-tuple-element.310) | copy-start | bytes 1179652
  167.2 103.7 %copy-start.35 = (f32[1536]{0:T(1024)S(1)}, f32[1536]{0:T(1024)}, u32[]{:S(2)}) copy-start(f32[1536]{0:T(1024)} %param.25) | copy-start | bytes 18436
  167.2 151.7 %all-gather.7.cloned.1.call-start = ((), (), s32[]{:S(2)}) async-start(), calls=%async_computation.6 | async-start | bytes 7864320 | tf_op jit(solution)/shard_map/all_gather | solution.py:148
  269.2 244.4 %copy-start.39 = (f32[512]{0:T(512)}, f32[512]{0:T(512)S(1)}, u32[]{:S(2)}) copy-start(f32[512]{0:T(512)S(1)} %add_rsqrt_fusion) | copy-start | bytes 6148
  272.4 94.4 %all-gather.9.cloned.1.call-start = ((), (), s32[]{:S(2)}) async-start(), calls=%async_computation.8 | async-start | bytes 7864320 | tf_op jit(solution)/shard_map/all_gather | solution.py:162
  273.0 236.3 %reduce-scatter.9.cloned.1.call-start = ((), (), s32[]{:S(2)}) async-start(), calls=%async_computation.9 | async-start | bytes 15728640 | tf_op jit(solution)/shard_map/reduce_scatter | solution.py:171
  318.9 12.6 copy-start.48
  318.9 12.6 copy-start.49
  366.8 18.8 %copy-start.50 = (bf16[1536,1024]{1,0:T(8,128)(2,1)S(1)}, bf16[1536,1024]{1,0:T(8,128)(2,1)}, u32[]{:S(2)}) copy-start(bf16[1536,1024]{1,0:T(8,128)(2,1)} %param.26) | copy-start | bytes 9437188
  385.5 11.6 copy-start.51
  385.5 11.6 copy-start.53
  410.1 154.0 %all-gather.11.cloned.1.call-start = ((), (), s32[]{:S(2)}) async-start(), calls=%async_computation.10 | async-start | bytes 7864320 | tf_op jit(solution)/shard_map/all_gather | solution.py:181
  517.5 436.8 %reduce-scatter.11.cloned.1.call-start = ((), (), s32[]{:S(2)}) async-start(), calls=%async_computation.11 | async-start | bytes 7864320 | tf_op jit(solution)/shard_map/reduce_scatter | solution.py:242
  616.2 12.2 copy-start.2
  684.3 12.2 copy-start.2
  753.0 12.2 copy-start.2
  821.6 12.2 copy-start.2
  868.4 14.7 %copy-start.20 = (bf16[2048,2,96]{0,2,1:T(8,128)(2,1)}, bf16[2048,2,96]{0,2,1:T(8,128)(2,1)S(1)}, u32[]{:S(2)}) copy-start(bf16[2048,2,96]{0,2,1:T(8,128)(2,1)S(1)} %convert_element_type.138) | copy-start | bytes 2359300
  895.8 120.9 %reduce-scatter.7.cloned.1.call-start = ((), (), s32[]{:S(2)}) async-start(), calls=%async_computation.7 | async-start | bytes 7864320 | tf_op jit(solution)/shard_map/reduce_scatter | solution.py:155
  906.8 530.3 %all-reduce.4.cloned.1.call-start = ((), (), s32[]{:S(2)}) async-start(), calls=%async_computation.12 | async-start | bytes 25952256 | tf_op jit(solution)/shard_map/psum | solution.py:256
  906.9 12.1 copy-start.52
  906.9 22.2 %slice-start.2 = ((s8[6291456]{0:T(1024)(128)(4,1)}), s8[4194304]{0:T(1024)(128)(4,1)S(1)}, s32[]{:S(2)}) async-start(s8[6291456]{0:T(1024)(128)(4,1)} %bitcast.262), calls=%async_computation.15 | async-start | bytes 8388608
  918.9 10.2 slice-start.3
  918.9 10.2 copy-start.54
  918.9 18.7 %slice-start = ((s8[6291456]{0:T(1024)(128)(4,1)}), s8[4194304]{0:T(1024)(128)(4,1)S(1)}, s32[]{:S(2)}) async-start(s8[6291456]{0:T(1024)(128)(4,1)} %bitcast.260), calls=%async_computation.13 | async-start | bytes 8388608
  929.1 8.6 copy-start.16
  950.4 66.3 %copy-start.36 = (f32[1536]{0:T(1024)S(1)}, f32[1536]{0:T(1024)}, u32[]{:S(2)}) copy-start(f32[1536]{0:T(1024)} %param.25) | copy-start | bytes 18436
  950.4 66.3 %copy-start.40 = (f32[512]{0:T(512)S(1)}, f32[512]{0:T(512)}, u32[]{:S(2)}) copy-start(f32[512]{0:T(512)} %copy-done.39) | copy-start | bytes 6148
  950.4 66.3 %copy-start.45 = (f32[512]{0:T(512)S(1)}, f32[512]{0:T(512)}, u32[]{:S(2)}) copy-start(f32[512]{0:T(512)} %copy-done.44) | copy-start | bytes 6148
  (47 other events, 204.7 us)
Sparse Core Ops, SparseCore 0:
  12.9 49.0 all-gather.4
  167.3 99.0 reduce-scatter.4
  272.5 46.3 all-gather.6
  320.3 46.3 all-gather.8
  410.2 99.0 reduce-scatter.8
  517.7 46.3 all-gather.10
  895.9 58.3 reduce-scatter.10
  957.6 59.0 reduce-scatter.6
  1023.5 413.5 all-reduce.3
where the time goes:
time: 1470 us; the launch traced here: 1460 us
  waiting for transfers between devices  801 us (54%)
  matrix products  336 us (23%)
  other arithmetic  136 us (9%)
  local copies, waits for them, and re-layouts  132 us (9%)
  blocking collectives  40.1 us (3%)
  between operations  14.9 us (1%)
    psum x1, waiting for transfers between devices, body(): lax.psum(grad_w_query.astype(jnp.bfloat16), 'dp').astype(jnp.float32)  413 us
    reduce_scatter x1, waiting for transfers between devices, body(): lax.psum_scatter(contract_cols(grad_gate, w_gate) + contract_cols(grad_up...  99.1 us
    reduce_scatter x1, waiting for transfers between devices, body(): lax.psum_scatter(jnp.dot(row_slice, w_out, preferred_element_type=jnp.flo...  99.1 us
    dot_general x7, matrix products, contract_cols(): lax.dot_general(left, right, (((1,), (1,)), ((), ())), preferred_element_...  76.6 us
    dynamic_update_slice x8, local copies, waits for them, and re-layouts, body(): lax.scan(attend_back, (zero_state, zero_state), (blocks_of_query, grad_bl...  71.2 us
    dot_general x4, matrix products, attend_back(): jnp.einsum('qgrd,kgd->grqk', grad_block, heads_of_value, preferred_elemen...  50.6 us
    convert_element_type x4, other arithmetic, attend_back(): grad_scores = (weights * (grad_weights - inner_sum)).astype(jnp.bfloat16)  48.7 us
    all_gather x1, waiting for transfers between devices, body(): lax.all_gather(grad_hidden_one.astype(jnp.bfloat16), 'tensor', axis=0, ti...  46.5 us
  transfers between devices with their start and end apart: 9, of which 9 were waited for; matrix products, arithmetic and copies ran while one was open for 6% of the time, Pallas kernels for 0%

commit v1 on v0

--- a/solution.py
+++ b/solution.py
@@ -253,7 +253,9 @@
     grad_tokens = grad_hidden_one + norm_back(grad_normed_one, norm_attn, unit_one, inverse_one)
     grad_norm_attn, grad_norm_mlp = lax.psum((grad_norm_attn, grad_norm_mlp), ("dp", "tensor"))
     grad_w_query, grad_w_key, grad_w_value, grad_w_out, grad_w_gate, grad_w_up, grad_w_down = (
-        lax.psum(grad_w_query.astype(jnp.bfloat16), "dp").astype(jnp.float32),
+        jnp.sum(lax.all_gather(grad_w_query.astype(jnp.bfloat16), "dp"), axis=0).astype(
+            jnp.float32
+        ),
         lax.psum(grad_w_key.astype(jnp.bfloat16), "dp").astype(jnp.float32),
         lax.psum(grad_w_value.astype(jnp.bfloat16), "dp").astype(jnp.float32),
         lax.psum(grad_w_out.astype(jnp.bfloat16), "dp").astype(jnp.float32),

time: 1470 us -> 1530 us (1.041)
  waiting for transfers between devices: 801 us -> 841 us
    all_gather x0 -> x1, waiting for transfers between devices: none -> 134 us  [body(): lax.all_gather(grad_w_query.astype(jnp.bfloat16), 'dp')]
    psum x1, waiting for transfers between devices: 413 us -> 312 us  [body(): lax.psum(grad_w_key.astype(jnp.bfloat16), 'dp').astype(jnp.float32)]
    reduce_scatter x1, waiting for transfers between devices: 3.95 us -> 42 us  [body(): lax.psum_scatter((contract_cols(grad_q_proj, w_query) + contract_cols(gra...]
    all_gather x1, waiting for transfers between devices: 46.5 us -> 16.4 us  [body(): lax.all_gather(grad_hidden_one.astype(jnp.bfloat16), 'tensor', axis=0, ti...]
  transfers between devices with their start and end apart: 9 -> 10, of which waited for: 9 -> 10; matrix products, arithmetic and copies ran while one was open for 6% -> 9% of each run, Pallas kernels for 0% -> 0%
where the time goes in v1:
time: 1530 us; the launch traced here: 1520 us
  waiting for transfers between devices  841 us (55%)
  matrix products  343 us (22%)
  other arithmetic  147 us (10%)
  local copies, waits for them, and re-layouts  131 us (9%)
  blocking collectives  40 us (3%)
    psum x1, waiting for transfers between devices, body(): lax.psum(grad_w_key.astype(jnp.bfloat16), 'dp').astype(jnp.float32)  312 us
    all_gather x1, waiting for transfers between devices, body(): lax.all_gather(grad_w_query.astype(jnp.bfloat16), 'dp')  134 us
    reduce_scatter x1, waiting for transfers between devices, body(): lax.psum_scatter(contract_cols(grad_gate, w_gate) + contract_cols(grad_up...  99.2 us
    reduce_scatter x1, waiting for transfers between devices, body(): lax.psum_scatter(jnp.dot(row_slice, w_out, preferred_element_type=jnp.flo...  99.1 us
    dot_general x7, matrix products, contract_cols(): lax.dot_general(left, right, (((1,), (1,)), ((), ())), preferred_element_...  77.2 us
    dynamic_update_slice x8, local copies, waits for them, and re-layouts, body(): lax.scan(attend_back, (zero_state, zero_state), (blocks_of_query, grad_bl...  71.2 us
    dot_general x4, matrix products, attend_back(): jnp.einsum('qgrd,kgd->grqk', grad_block, heads_of_value, preferred_elemen...  50.4 us
    dot_general x7, matrix products, contract_rows(): lax.dot_general(left, right, (((0,), (0,)), ((), ())), preferred_element_...  49.4 us
  transfers between devices with their start and end apart: 10, of which 10 were waited for; matrix products, arithmetic and copies ran while one was open for 9% of the time, Pallas kernels for 0%

profile of v1, /device:TPU:0, one launch (start us, length us, event | category | flops | bytes accessed | tf_op | source)
XLA Modules:
  0.0 1518.1 jit_solution(14227580577126438357)
XLA Ops:
  15.7 46.3 %all-gather.7.cloned.1.call-done = bf16[2048,1536]{1,0:T(8,128)(2,1)} async-done(((bf16[512,1536]{1,0:T(8,128)(2,1)}), bf16[2048,1536]{1,0:T(8,128)(2,1)}) %all-gather.7.cloned.1.call-update) | async-done | bytes 6291472 | tf_op jit(solution)/shard_map/all_gather | solution.py:104
  89.8 66.5 %while.28 = (s32[]{:T(128)}, bf16[4,512,2,2,96]{1,4,3,2,0:T(8,128)(2,1)}, f32[4,2,2,512]{3,2,1,0:T(2,128)}, s32[4,512]{1,0:T(4,128)S(1)}, s32[2048]{0:T(1024)S(1...) while((s32[]{:T(128)}, ...), condition=%wide.region_4.5_spmd.clone, body=%wide.region_1.4_spmd.clone.sunk | while | flops 1664284672 | bytes 60117144 | solution.py:135
  167.1 99.1 %reduce-scatter.5.cloned.1.call-done = f32[512,1536]{1,0:T(8,128)} async-done(((f32[2048,1536]{1,0:T(8,128)}), f32[512,1536]{1,0:T(8,128)}) %reduce-scatter.5.cloned.1.call-update) | async-done | bytes 3145744 | tf_op jit(solution)/shard_map/reduce_scatter | solution.py:138
  272.9 45.9 %all-gather.9.cloned.1.call-done = bf16[2048,1536]{1,0:T(8,128)(2,1)} async-done(((bf16[512,1536]{1,0:T(8,128)(2,1)}), bf16[2048,1536]{1,0:T(8,128)(2,1)}) %all-gather.9.cloned.1.call-update) | async-done | bytes 6291472 | tf_op jit(solution)/shard_map/all_gather | solution.py:148
  318.8 12.6 fusion.74
  340.2 26.4 %all-gather.11.cloned.1.call-done = bf16[2048,1536]{1,0:T(8,128)(2,1)} async-done(((bf16[512,1536]{1,0:T(8,128)(2,1)}), bf16[2048,1536]{1,0:T(8,128)(2,1)}) %all-gather.11.cloned.1.call-update) | async-done | bytes 6291472 | tf_op jit(solution)/shard_map/all_gather | solution.py:162
  366.7 18.8 %multiply_convert_fusion = (bf16[2048,1024]{1,0:T(8,128)(2,1)}, bf16[2048,1024]{1,0:T(8,128)(2,1)}, bf16[2048,1024]{1,0:T(8,128)(2,1)}) fusion(f32[2048,1024]{1,0:T(8,128)} %fusion.73, f32[2048,1024]{1,0:T(8,128)} %fusion.74, bf16[2048,1536]{1,0:T(8,128)(2,1)} %all-gather.11.cloned.1.call-done, bf16[1024,1536]{1,0:T(8,128)(2,1)S(1)} %copy-done), kind=kOutput, calls=%fused_computation.69 | convolution fusion | flops 6473908224 | bytes 38797312 | tf_op jit(solution)/shard_map/dot_general | solution.py:61
  385.5 11.9 fusion.75
  397.4 13.1 convolution_add_fusion
  410.6 99.2 %reduce-scatter.9.cloned.1.call-done = f32[512,1536]{1,0:T(8,128)} async-done(((f32[2048,1536]{1,0:T(8,128)}), f32[512,1536]{1,0:T(8,128)}) %reduce-scatter.9.cloned.1.call-update) | async-done | bytes 3145744 | tf_op jit(solution)/shard_map/reduce_scatter | solution.py:171
  518.1 11.4 convolution_convert_fusion.2
  548.1 16.4 %all-gather.13.cloned.1.call-done = bf16[2048,1536]{1,0:T(8,128)(2,1)} async-done(((bf16[512,1536]{1,0:T(8,128)(2,1)}), bf16[2048,1536]{1,0:T(8,128)(2,1)}) %all-gather.13.cloned.1.call-update) | async-done | bytes 6291472 | tf_op jit(solution)/shard_map/all_gather | solution.py:181
  585.2 273.6 %while.29 = (s32[]{:T(128)}, f32[2048,2,96]{0,2,1:T(8,128)}, f32[2048,2,96]{0,2,1:T(8,128)}, f32[4,512,2,2,96]{1,0,4,3,2:T(4,128)}, bf16[4,512,2,2,96]{1,4,3,2,0...) while((s32[]{:T(128)}, f32[2048,2,96]{0,2,1:T(8,128)}, ...), condition=%wide.region_12.13_spmd.clone, body=%wide.region_10.12_spmd.clone.sunk | while | flops 4094752768 | bytes 214511840 | solution.py:222
  604.0 12.6 fusion.155
  616.6 12.2 fusion.156
  637.0 16.1 %dynamic_update_slice.22 = f32[4,512,2,2,96]{1,0,4,3,2:T(4,128)} dynamic-update-slice(f32[4,512,2,2,96]{1,0,4,3,2:T(4,128)} %get-tuple-element.502, f32[1,512,2,2,96]{1,0,4,3,2:T(1,128)} %copy.49, s32[]{:T(128)S(6)} %copy.66, s32[]{:T(128)} %constant.59.clone.1..sunk, s32[]{:T(128)} %constant.59.clone.1..sunk, s32[]{:T(128)} %constant.59.clone.1..sunk, s32[]{:T(128)} %constant.59.clone.1..sunk) | dynamic-update-slice | bytes 1572868 | tf_op jit(solution)/shard_map/while/body/jit(dynamic_update_index_in_dim)/dynamic_update_slice | solution.py:222
  672.0 12.6 fusion.155
  684.6 12.2 fusion.156
  705.5 16.1 %dynamic_update_slice.22 = f32[4,512,2,2,96]{1,0,4,3,2:T(4,128)} dynamic-update-slice(f32[4,512,2,2,96]{1,0,4,3,2:T(4,128)} %get-tuple-element.502, f32[1,512,2,2,96]{1,0,4,3,2:T(1,128)} %copy.49, s32[]{:T(128)S(6)} %copy.66, s32[]{:T(128)} %constant.59.clone.1..sunk, s32[]{:T(128)} %constant.59.clone.1..sunk, s32[]{:T(128)} %constant.59.clone.1..sunk, s32[]{:T(128)} %constant.59.clone.1..sunk) | dynamic-update-slice | bytes 1572868 | tf_op jit(solution)/shard_map/while/body/jit(dynamic_update_index_in_dim)/dynamic_update_slice | solution.py:222
  740.6 12.6 fusion.155
  753.2 12.2 fusion.156
  774.0 16.1 %dynamic_update_slice.22 = f32[4,512,2,2,96]{1,0,4,3,2:T(4,128)} dynamic-update-slice(f32[4,512,2,2,96]{1,0,4,3,2:T(4,128)} %get-tuple-element.502, f32[1,512,2,2,96]{1,0,4,3,2:T(1,128)} %copy.49, s32[]{:T(128)S(6)} %copy.66, s32[]{:T(128)} %constant.59.clone.1..sunk, s32[]{:T(128)} %constant.59.clone.1..sunk, s32[]{:T(128)} %constant.59.clone.1..sunk, s32[]{:T(128)} %constant.59.clone.1..sunk) | dynamic-update-slice | bytes 1572868 | tf_op jit(solution)/shard_map/while/body/jit(dynamic_update_index_in_dim)/dynamic_update_slice | solution.py:222
  809.1 12.6 fusion.155
  821.7 12.2 fusion.156
  842.6 16.1 %dynamic_update_slice.22 = f32[4,512,2,2,96]{1,0,4,3,2:T(4,128)} dynamic-update-slice(f32[4,512,2,2,96]{1,0,4,3,2:T(4,128)} %get-tuple-element.502, f32[1,512,2,2,96]{1,0,4,3,2:T(1,128)} %copy.49, s32[]{:T(128)S(6)} %copy.66, s32[]{:T(128)} %constant.59.clone.1..sunk, s32[]{:T(128)} %constant.59.clone.1..sunk, s32[]{:T(128)} %constant.59.clone.1..sunk, s32[]{:T(128)} %constant.59.clone.1..sunk) | dynamic-update-slice | bytes 1572868 | tf_op jit(solution)/shard_map/while/body/jit(dynamic_update_index_in_dim)/dynamic_update_slice | solution.py:222
  895.0 12.7 add_convert_fusion
  907.8 11.2 convolution_convert_fusion
  926.9 312.3 %all-reduce.4.cloned.1.call-done = (bf16[1536,192]{0,1:T(8,128)(2,1)}, bf16[1536,192]{0,1:T(8,128)(2,1)}, bf16[384,1536]{1,0:T(8,128)(2,1)}, bf16[1536,1024]{1,0...) async-done(((bf16[1536,192]{0,1:T(8,128)(2,1)}, bf16[1536,192]{0,1:T(8,128)(2,1)}, bf16[384,1536]{1,0:T(8,128)(2,1)}, bf16[1536,1024]{1,0:T(8,128)(2,1)}, ...) | async-done | bytes 11796496 | tf_op jit(solution)/shard_map/psum | solution.py:259
  1257.2 42.0 %reduce-scatter.11.cloned.1.call-done = bf16[512,1536]{1,0:T(8,128)(2,1)} async-done(((bf16[2048,1536]{1,0:T(8,128)(2,1)}), bf16[512,1536]{1,0:T(8,128)(2,1)}) %reduce-scatter.11.cloned.1.call-update) | async-done | bytes 1572880 | tf_op jit(solution)/shard_map/reduce_scatter | solution.py:242
  1302.2 40.0 %all-reduce = (f32[1536]{0:T(1024)}, f32[1536]{0:T(1024)}) all-reduce(f32[1536]{0:T(1024)S(1)} %get-tuple-element.234, f32[1536]{0:T(1024)S(1)} %copy-done.37), channel_id=1, replica_groups=mesh['dp'=8,'tensor'=4] {'dp','tensor'}, use_global_device_ids=true, to_apply=%region_16.17 | all-reduce | flops 3072 | bytes 24576 | tf_op jit(solution)/shard_map/psum | solution.py:254
  1342.2 18.7 %reduce-scatter.7.cloned.1.call-done = bf16[512,1536]{1,0:T(8,128)(2,1)} async-done(((bf16[2048,1536]{1,0:T(8,128)(2,1)}), bf16[512,1536]{1,0:T(8,128)(2,1)}) %reduce-scatter.7.cloned.1.call-update) | async-done | bytes 1572880 | tf_op jit(solution)/shard_map/reduce_scatter | solution.py:155
  1367.8 134.0 %all-gather.15.cloned.1.call-done = bf16[12288,384]{1,0:T(8,128)(2,1)} async-done(((bf16[1536,384]{1,0:T(8,128)(2,1)}), bf16[12288,384]{1,0:T(8,128)(2,1)}) %all-gather.15.cloned.1.call-update) | async-done | bytes 9437200 | tf_op jit(solution)/shard_map/all_gather | solution.py:256
  (267 shorter events, 366.7 us)
Async XLA Ops:
  7.2 359.5 %copy-start = (bf16[1024,1536]{1,0:T(8,128)(2,1)S(1)}, bf16[1024,1536]{1,0:T(8,128)(2,1)}, u32[]{:S(2)}) copy-start(bf16[1024,1536]{1,0:T(8,128)(2,1)} %param.28) | copy-start | bytes 9437188
  7.2 54.8 %all-gather.7.cloned.1.call-start = ((), (), s32[]{:S(2)}) async-start(), calls=%async_computation.4 | async-start | bytes 7864320 | tf_op jit(solution)/shard_map/all_gather | solution.py:104
  12.8 253.5 %reduce-scatter.5.cloned.1.call-start = ((), (), s32[]{:S(2)}) async-start(), calls=%async_computation.5 | async-start | bytes 15728640 | tf_op jit(solution)/shard_map/reduce_scatter | solution.py:138
  15.7 55.7 %copy-start.7 = (f32[2048,48]{0,1:T(8,128)}, f32[2048,48]{0,1:T(8,128)S(1)}, u32[]{:S(2)}) copy-start(f32[2048,48]{0,1:T(8,128)S(1)} %get-tuple-element.309) | copy-start | bytes 1179652
  167.1 103.8 %copy-start.31 = (f32[1536]{0:T(1024)S(1)}, f32[1536]{0:T(1024)}, u32[]{:S(2)}) copy-start(f32[1536]{0:T(1024)} %param.25) | copy-start | bytes 18436
  167.1 151.8 %all-gather.9.cloned.1.call-start = ((), (), s32[]{:S(2)}) async-start(), calls=%async_computation.6 | async-start | bytes 7864320 | tf_op jit(solution)/shard_map/all_gather | solution.py:148
  269.1 245.0 %copy-start.35 = (f32[512]{0:T(512)}, f32[512]{0:T(512)S(1)}, u32[]{:S(2)}) copy-start(f32[512]{0:T(512)S(1)} %add_rsqrt_fusion) | copy-start | bytes 6148
  272.3 94.4 %all-gather.11.cloned.1.call-start = ((), (), s32[]{:S(2)}) async-start(), calls=%async_computation.8 | async-start | bytes 7864320 | tf_op jit(solution)/shard_map/all_gather | solution.py:162
  272.9 236.9 %reduce-scatter.9.cloned.1.call-start = ((), (), s32[]{:S(2)}) async-start(), calls=%async_computation.9 | async-start | bytes 15728640 | tf_op jit(solution)/shard_map/reduce_scatter | solution.py:171
  318.8 12.6 copy-start.44
  318.8 12.6 copy-start.45
  366.7 18.8 %copy-start.46 = (bf16[1536,1024]{1,0:T(8,128)(2,1)S(1)}, bf16[1536,1024]{1,0:T(8,128)(2,1)}, u32[]{:S(2)}) copy-start(bf16[1536,1024]{1,0:T(8,128)(2,1)} %param.26) | copy-start | bytes 9437188
  385.4 11.9 copy-start.47
  385.5 11.9 copy-start.49
  410.5 154.0 %all-gather.13.cloned.1.call-start = ((), (), s32[]{:S(2)}) async-start(), calls=%async_computation.10 | async-start | bytes 7864320 | tf_op jit(solution)/shard_map/all_gather | solution.py:181
  518.0 721.1 %all-reduce.4.cloned.1.call-start = ((), (), s32[]{:S(2)}) async-start(), calls=%async_computation.13 | async-start | bytes 23592960 | tf_op jit(solution)/shard_map/psum | solution.py:259
  518.1 11.4 copy-start.48
  518.1 21.6 %slice-start.2 = ((s8[6291456]{0:T(1024)(128)(4,1)}), s8[4194304]{0:T(1024)(128)(4,1)S(1)}, s32[]{:S(2)}) async-start(s8[6291456]{0:T(1024)(128)(4,1)} %bitcast.264), calls=%async_computation.16 | async-start | bytes 8388608
  529.5 10.1 copy-start.50
  616.6 12.2 copy-start.2
  684.6 12.2 copy-start.2
  753.2 12.2 copy-start.2
  821.7 12.2 copy-start.2
  873.1 426.1 %reduce-scatter.11.cloned.1.call-start = ((), (), s32[]{:S(2)}) async-start(), calls=%async_computation.11 | async-start | bytes 7864320 | tf_op jit(solution)/shard_map/reduce_scatter | solution.py:242
  907.8 453.0 %reduce-scatter.7.cloned.1.call-start = ((), (), s32[]{:S(2)}) async-start(), calls=%async_computation.7 | async-start | bytes 7864320 | tf_op jit(solution)/shard_map/reduce_scatter | solution.py:155
  919.0 582.8 %all-gather.15.cloned.1.call-start = ((), (), s32[]{:S(2)}) async-start(), calls=%async_computation.12 | async-start | bytes 10616832 | tf_op jit(solution)/shard_map/all_gather | solution.py:256
  1253.6 45.6 %copy-start.34 = (f32[1536]{0:T(1024)S(1)}, f32[1536]{0:T(1024)}, u32[]{:S(2)}) copy-start(f32[1536]{0:T(1024)} %param.20) | copy-start | bytes 18436
  1253.6 45.6 %copy-start.39 = (f32[512]{0:T(512)S(1)}, f32[512]{0:T(512)}, u32[]{:S(2)}) copy-start(f32[512]{0:T(512)} %copy-done.38) | copy-start | bytes 6148
  1257.2 44.9 %copy-start.37 = (f32[1536]{0:T(1024)S(1)}, f32[1536]{0:T(1024)}, u32[]{:S(2)}) copy-start(f32[1536]{0:T(1024)} %get-tuple-element.232) | copy-start | bytes 18436
  1257.2 103.6 %copy-start.32 = (f32[1536]{0:T(1024)S(1)}, f32[1536]{0:T(1024)}, u32[]{:S(2)}) copy-start(f32[1536]{0:T(1024)} %param.25) | copy-start | bytes 18436
  1257.2 103.6 %copy-start.36 = (f32[512]{0:T(512)S(1)}, f32[512]{0:T(512)}, u32[]{:S(2)}) copy-start(f32[512]{0:T(512)} %copy-done.35) | copy-start | bytes 6148
  1257.2 103.6 %copy-start.41 = (f32[512]{0:T(512)S(1)}, f32[512]{0:T(512)}, u32[]{:S(2)}) copy-start(f32[512]{0:T(512)} %copy-done.40) | copy-start | bytes 6148
  (42 other events, 205.5 us)
Sparse Core Ops, SparseCore 0:
  12.9 49.0 all-gather.6
  167.2 99.0 reduce-scatter.4
  272.4 46.3 all-gather.8
  320.3 46.3 all-gather.10
  410.7 99.0 reduce-scatter.8
  518.2 46.3 all-gather.12
  873.2 365.8 all-reduce.3
  1241.9 57.2 reduce-scatter.10
  1301.7 59.0 reduce-scatter.6
  1363.7 138.0 all-gather.14
